TPU v7x, 512 devices: a whole 4x8x8 slice. The times are simulated.
512 devices in a mesh: pool: 32 (over z_hi, y), ctx: 4 (over x), head: 4 (over z_lo, core).
Axes of the slice: x: 4, y: 8, z: 8 (z_hi: 4, z_lo: 2; z = z_hi * 2 + z_lo), core: 2. Of those that a mesh axis runs over, the one named last changes fastest.
Arguments:
- kv_pool: bfloat16 [4, 1024, 2, 32, 1024], P('ctx', 'pool', None, None, 'head'), may hold values from -6 to 6
- state_pool: bfloat16 [1024, 64, 1024], P('pool', 'ctx', 'head'), may hold values from -0.59765625 to 0.59765625
- block_owner: int32 [4, 1024], P('ctx'), may hold values from 0 to 31, as said below
- block_index: int32 [4, 1024], P('ctx'), may hold values from 0 to 31, as said below
- history_len: int32 [32], P('pool'), may hold values from 1 to 4096, as said below
- turn_len: int32 [32], P('pool'), may hold values from 256 to 512, as said below
- mixer_in: bfloat16 [32, 128, 64, 512], P('pool', 'head', 'ctx'), may hold values from -6 to 6
- input_proj: bfloat16 [32, 8, 256, 512], P('pool', 'head'), may hold values from -1.5 to 1.5
- output_proj: bfloat16 [32, 8, 256, 512], P('pool', 'head'), may hold values from -6 to 6
- step_size: float32 [32, 128, 512], P('pool', 'head'), may hold values from 0 to 2, as said below
- decay_rate: float32 [128], P('head'), may hold values from 0 to 4, as said below
- bypass_factor: float32 [128], P('head'), may hold values from 0.5 to 1.5
- queries: bfloat16 [32, 512, 8192], P('pool', 'ctx', 'head'), may hold values from -300 to 300
- turn_kv: bfloat16 [32, 2, 512, 1024], P('pool', None, 'ctx', 'head'), may hold values from -6 to 6
Outputs:
- mixer_out: bfloat16 [32, 128, 64, 512], P('pool', 'head', 'ctx')
- next_state: float32 [32, 128, 64, 256], P('pool', 'head', 'ctx')
- attn_out: bfloat16 [32, 512, 8192], P('pool', 'ctx', 'head')
Inputs may be any that keep to these rules, and one draw needn't show every extreme that they name: `block_owner`: in each row c, every session owns exactly 32 slots, and each aligned run of 32 slots (one pool shard) holds at most 2 blocks of any one session; in every row some shard holds exactly 2 blocks of some session. `block_index`: in each row, the slots of one session carry the indices 0 to 31, each once. `history_len`: some session has exactly 4096. `turn_len`: every value is at least 256 and some session has exactly 512. `step_size`: Positive. `decay_rate`: Positive.
All inputs are finite; a program needn't handle non-finite values.
Results may differ from a plain program's by a relative error of at most 0.008.
Values may be sent and summed in bfloat16 or wider, within the bound.
A program may use at most 64 MiB of HBM per device.

v0:
```python
import jax
import jax.numpy as jnp
from jax import lax
from jax.sharding import PartitionSpec as P

Q_HEADS = 64
KV_HEADS = 8
HEAD_DIM = 128
PAGE = 32
BLK = 128
floor_score = -1e30


def spanned_ssd(
    values, input_proj, output_proj, step_sizes, rates, bypass_factor, start_state, valid_len
):
    heads, channels, total = values.shape
    groups = input_proj.shape[0]
    per_group = heads // groups
    count = total // BLK
    positions = jnp.arange(total, dtype=jnp.int32)
    live = positions < valid_len
    step_sizes = jnp.where(live[None, :], step_sizes, jnp.float32(0.0))
    value_blocks = values.reshape(heads, channels, count, BLK).transpose(2, 0, 1, 3)
    input_blocks = input_proj.reshape(groups, -1, count, BLK).transpose(2, 0, 1, 3)
    output_blocks = output_proj.reshape(groups, -1, count, BLK).transpose(2, 0, 1, 3)
    step_blocks = step_sizes.reshape(heads, count, BLK).transpose(1, 0, 2)
    offsets = jnp.arange(BLK, dtype=jnp.int32)
    lower = offsets[:, None] >= offsets[None, :]
    exact = lax.Precision.HIGHEST

    def advance(carried, item):
        value_blk, input_blk, output_blk, step_blk = item
        value_blk = value_blk.astype(jnp.float32)
        input_blk = input_blk.astype(jnp.float32)
        output_blk = output_blk.astype(jnp.float32)
        running = jnp.cumsum(-rates[:, None] * step_blk, axis=1)
        pairs = jnp.einsum("gnt,gns->gts", output_blk, input_blk, precision=exact)
        pairs = jnp.repeat(pairs, per_group, axis=0)
        gaps = jnp.minimum(running[:, :, None] - running[:, None, :], 0.0)
        mixing = jnp.where(lower[None], jnp.exp(gaps), 0.0) * pairs * step_blk[:, None, :]
        result = jnp.einsum("hts,hps->hpt", mixing, value_blk, precision=exact)
        read_out = jnp.repeat(output_blk, per_group, axis=0)
        result = result + jnp.exp(running)[:, None, :] * jnp.einsum(
            "hpn,hnt->hpt", carried, read_out, precision=exact
        )
        result = result + bypass_factor[:, None, None] * value_blk
        weights = jnp.exp(running[:, -1:] - running) * step_blk
        write_in = jnp.repeat(input_blk, per_group, axis=0)
        carried = jnp.exp(running[:, -1])[:, None, None] * carried + jnp.einsum(
            "hps,hns->hpn", value_blk * weights[:, None, :], write_in, precision=exact
        )
        return (carried, result)

    final_state, results = lax.scan(
        advance, start_state, (value_blocks, input_blocks, output_blocks, step_blocks)
    )
    results = results.transpose(1, 2, 0, 3).reshape(heads, channels, total)
    return (jnp.where(live[None, None, :], results, 0.0), final_state)


def route_blocks(kv_local, state_local, owner_row, index_row):
    parties = lax.axis_size("pool")
    myself = lax.axis_index("pool")
    pages = kv_local.shape[1]
    capacity = 2 * pages // parties
    sessions = jnp.arange(parties, dtype=jnp.int32)
    table = (
        (owner_row[:, None] == sessions[None, :]).astype(jnp.int32).reshape(parties, pages, parties)
    )
    before = jnp.cumsum(table, axis=1) - table
    ranks = jnp.sum(before * table, axis=2)
    owners = owner_row.reshape(parties, pages)
    my_owner = lax.dynamic_index_in_dim(owners, myself, 0, keepdims=False)
    device_rank = lax.dynamic_index_in_dim(ranks, myself, 0, keepdims=False)
    send_kv = (
        jnp.zeros((parties, capacity) + kv_local.shape[2:], kv_local.dtype)
        .at[my_owner, device_rank]
        .set(kv_local[0])
    )
    send_state = (
        jnp.zeros((parties, capacity) + state_local.shape[1:], state_local.dtype)
        .at[my_owner, device_rank]
        .set(state_local)
    )
    recv_kv, recv_state = (
        lax.all_to_all(send_kv, "pool", split_axis=0, concat_axis=0, tiled=True),
        lax.all_to_all(send_state, "pool", split_axis=0, concat_axis=0, tiled=True),
    )
    flat_place = (sessions[:, None] * capacity + ranks).reshape(-1)
    target = jnp.where(owner_row == myself, index_row, pages)
    where_from = jnp.zeros((pages,), jnp.int32).at[target].set(flat_place, mode="drop")
    hist_pages = recv_kv.reshape((parties * capacity,) + recv_kv.shape[2:])[where_from]
    start_slabs = recv_state.reshape((parties * capacity,) + recv_state.shape[2:])[where_from]
    return (hist_pages, start_slabs)


def attend_block(carried, query_rows, query_index, block, seg_id, hist_rows, history_len):
    rows = query_rows.shape[0]
    key_rows = block.shape[1]
    width = block.shape[2]
    groups = width // HEAD_DIM
    per_group = Q_HEADS // KV_HEADS
    turn_rows = key_rows - hist_rows
    offsets = jnp.arange(key_rows, dtype=jnp.int32)
    in_history = offsets < hist_rows
    placed = jnp.where(
        in_history, seg_id * hist_rows + offsets, seg_id * turn_rows + offsets - hist_rows
    )
    seen_mask = jnp.where(
        in_history[None, :],
        (placed < history_len)[None, :],
        placed[None, :] <= query_index[:, None],
    )
    score_scale = HEAD_DIM ** (-0.5)
    peak, totals, summed = carried
    query_heads = query_rows.reshape(rows, groups, per_group, HEAD_DIM)
    key_heads = block[0].reshape(key_rows, groups, HEAD_DIM)
    value_heads = block[1].reshape(key_rows, groups, HEAD_DIM)
    scores = (
        jnp.einsum("rgqd,kgd->rgqk", query_heads, key_heads, preferred_element_type=jnp.float32)
        * score_scale
    )
    mask = seen_mask[:, None, None, :]
    fresh = jnp.maximum(peak, jnp.max(jnp.where(mask, scores, floor_score), axis=-1))
    weights = jnp.where(mask, jnp.exp(scores - fresh[..., None]), 0.0)
    fade = jnp.exp(peak - fresh)
    totals = fade * totals + jnp.sum(weights, axis=-1)
    summed = fade[..., None] * summed + jnp.einsum(
        "rgqk,kgd->rgqd",
        weights.astype(jnp.bfloat16),
        value_heads,
        preferred_element_type=jnp.float32,
    )
    return (fresh, totals, summed)


def context_attention(query_rows, history, turn_keys, history_len, turn_len):
    turn_rows = query_rows.shape[0]
    hist_rows = history.shape[1]
    seg_rows = hist_rows + turn_rows
    width = history.shape[-1]
    groups = width // HEAD_DIM
    per_group = Q_HEADS // KV_HEADS
    segment = lax.axis_index("ctx")
    local_keys = jnp.concatenate([history, turn_keys], axis=1)
    row_ids = jnp.arange(turn_rows, dtype=jnp.int32)
    own_index = segment * turn_rows + row_ids
    carried = (
        jnp.full((turn_rows, groups, per_group), floor_score, jnp.float32),
        jnp.zeros((turn_rows, groups, per_group), jnp.float32),
        jnp.zeros((turn_rows, groups, per_group, HEAD_DIM), jnp.float32),
    )
    piece = lax.all_gather(local_keys, "ctx", axis=1, tiled=True)
    count = piece.shape[1] // seg_rows
    blocks = piece.reshape(2, count, seg_rows, width).transpose(1, 0, 2, 3)

    def visit(inner, item):
        block, offset = item
        return (
            attend_block(inner, query_rows, own_index, block, offset, hist_rows, history_len),
            None,
        )

    carried, _ = lax.scan(visit, carried, (blocks, jnp.arange(count, dtype=jnp.int32)))
    peak, totals, summed = carried
    result = (summed / totals[..., None]).reshape(turn_rows, groups * per_group * HEAD_DIM)
    return jnp.where((own_index < turn_len)[:, None], result, 0.0).astype(jnp.bfloat16)


def local(
    kv_pool,
    state_pool,
    block_owner,
    block_index,
    history_len,
    turn_len,
    mixer_in,
    input_proj,
    output_proj,
    step_size,
    decay_rate,
    bypass_factor,
    queries,
    turn_kv,
):
    hist_pages, start_slabs = route_blocks(kv_pool, state_pool, block_owner[0], block_index[0])
    pages = hist_pages.shape[0]
    width = hist_pages.shape[-1]
    history = hist_pages.transpose(1, 0, 2, 3).reshape(2, pages * PAGE, width)
    mixed, final = spanned_ssd(
        mixer_in[0],
        input_proj[0],
        output_proj[0],
        step_size[0],
        decay_rate,
        bypass_factor,
        start_slabs.astype(jnp.float32),
        turn_len[0],
    )
    attended = context_attention(queries[0], history, turn_kv[0], history_len[0], turn_len[0])
    return (mixed.astype(jnp.bfloat16)[None], final[None], attended[None])


def solution(mesh):
    return jax.shard_map(
        local,
        mesh=mesh,
        in_specs=(
            P("ctx", "pool", None, None, "head"),
            P("pool", "ctx", "head"),
            P("ctx", None),
            P("ctx", None),
            P("pool"),
            P("pool"),
            P("pool", "head", "ctx", None),
            P("pool", "head", None, None),
            P("pool", "head", None, None),
            P("pool", "head", None),
            P("head"),
            P("head"),
            P("pool", "ctx", "head"),
            P("pool", None, "ctx", "head"),
        ),
        out_specs=(
            P("pool", "head", "ctx", None),
            P("pool", "head", "ctx", None),
            P("pool", "ctx", "head"),
        ),
        check_vma=False,
    )
```

profile of v0, /device:TPU:1, one launch (start us, length us, event | category | flops | bytes accessed | tf_op | source)
XLA Modules:
  0.0 286.1 jit_solution(10285035328454896795)
XLA Ops:
  7.7 1.3 reduce.7
  9.2 1.0 fusion.51
  10.4 0.9 broadcast_in_dim.176
  11.3 4.3 %scatter_fusion = bf16[32,2,16,256]{3,2,1,0:T(8,128)(2,1)} fusion(bf16[32,2,16,256]{3,2,1,0:T(8,128)(2,1)} %broadcast_in_dim.176, s32[32]{0:T(128)S(1)} %fusion.47, bf16[32,16,256]{2,1,0:T(8,128)(2,1)} %param.19), kind=kCustom, calls=%fused_computation.2 | custom fusion | bytes 786688 | tf_op jit(solution)/shard_map/scatter | solution.py:84
  15.6 16.5 %all-to-all-start = ((bf16[32,2,16,256]{3,2,1,0:T(8,128)(2,1)}), bf16[32,2,16,256]{3,2,1,0:T(8,128)(2,1)S(1)}, u32[]{:S(2)}, u32[]{:S(2)}) async-start(bf16[32,2,16,256]{3,2,1,0:T(8,128)(2,1)} %scatter_fusion), calls=%async_computation | async-start | bytes 1048576 | tf_op jit(solution)/shard_map/all_to_all | solution.py:88
  32.1 1.6 broadcast_in_dim.189
  33.7 5.0 %scatter_fusion.1 = bf16[32,2,2,32,256]{4,3,2,1,0:T(8,128)(2,1)} fusion(bf16[32,2,2,32,256]{4,3,2,1,0:T(8,128)(2,1)} %broadcast_in_dim.189, s32[32]{0:T(128)S(1)} %fusion.47, bf16[32,2,32,256]{3,2,1,0:T(8,128)(2,1)S(1)} %bitcast.210), kind=kCustom, calls=%fused_computation.4 | custom fusion | bytes 3145984 | tf_op jit(solution)/shard_map/scatter | solution.py:79
  38.7 9.7 %all-to-all-done = bf16[32,2,16,256]{3,2,1,0:T(8,128)(2,1)S(1)} async-done(((bf16[32,2,16,256]{3,2,1,0:T(8,128)(2,1)}), bf16[32,2,16,256]{3,2,1,0:T(8,128)(2,1)S(1)}, u32[]{:S(2)}, u32[]{:S(2)}) %all-to-all-start) | async-done | bytes 524320 | tf_op jit(solution)/shard_map/all_to_all | solution.py:88
  48.4 8.1 %all-to-all-start.1 = ((bf16[32,2,2,32,256]{4,3,2,1,0:T(8,128)(2,1)}), bf16[32,2,2,32,256]{4,3,2,1,0:T(8,128)(2,1)}, u32[]{:S(2)}, u32[]{:S(2)}) async-start(bf16[32,2,2,32,256]{4,3,2,1,0:T(8,128)(2,1)} %scatter_fusion.1), calls=%async_computation.1 | async-start | bytes 4194304 | tf_op jit(solution)/shard_map/all_to_all | solution.py:87
  58.2 4.5 %scatter_custom_fusion.1 = s32[32]{0:T(128)S(1)} fusion(s32[1024]{0:T(1024)S(1)} %bitcast.214, s32[1024]{0:T(1024)S(1)} %reshape.369, s32[]{:T(128)} %constant.117.clone.1), kind=kCustom, calls=%fused_computation.95 | custom fusion | bytes 132 | tf_op jit(solution)/shard_map/scatter | solution.py:92
  64.5 49.6 %all-to-all-done.1 = bf16[32,2,2,32,256]{4,3,2,1,0:T(8,128)(2,1)} async-done(((bf16[32,2,2,32,256]{4,3,2,1,0:T(8,128)(2,1)}), bf16[32,2,2,32,256]{4,3,2,1,0:T(8,128)(2,1)}, u32[]{:S(2)}, u32[]{:S(2)}) %all-to-all-start.1) | async-done | bytes 2097184 | tf_op jit(solution)/shard_map/all_to_all | solution.py:87
  114.1 3.2 %gather_fusion.1 = bf16[32,2,32,256]{3,2,1,0:T(8,128)(2,1)} fusion(bf16[64,2,32,256]{3,2,1,0:T(8,128)(2,1)} %bitcast.17, s32[1024]{0:T(1024)S(1)} %pad_clamp_fusion), kind=kCustom, calls=%fused_computation.1 | custom fusion | bytes 2097280 | tf_op jit(solution)/shard_map/gather | solution.py:93
  117.3 1.3 copy.80
  118.6 1.1 pad_maximum_fusion
  119.7 52.2 %while.32 = (s32[]{:T(128)}, f32[32,16,256]{2,1,0:T(8,128)S(1)}, bf16[4,32,16,128]{3,2,1,0:T(8,128)(2,1)}, f32[32,1]{0,1:T(1,128)S(1)}, f32[4,32,128]{2,0,1:T(4,...) while((s32[]{:T(128)}, f32[32,16,256]{2,1,0:T(8,128)S(1)}, ...), condition=%wide.region_6.7_spmd.clone, body=%wide.region_4.6_spmd.clone.sunk | while | flops 524115968 | bytes 31068848 | solution.py:55
  121.0 1.7 fusion.87
  124.6 3.1 %fusion.88 = bf16[4,32,16,128]{3,2,1,0:T(8,128)(2,1)S(1)} fusion(bf16[4,32,16,128]{3,2,1,0:T(8,128)(2,1)S(1)} %copy-done.8, s32[]{:T(128)} %get-tuple-element.550, f32[32,16,128]{2,1,0:T(8,128)S(1)} %fusion.87, f32[32,256,128]{2,1,0:T(8,128)S(1)} %bitcast.192, f32[32,16,256]{2,1,0:T(8,128)S(1)} %get-tuple-element.551, f32[32]{0:T(128)} %get-tuple-element.569, ...), kind=kOutput, calls=%fused_computation.42.clone.1 | convolution fusion | flops 201654272 | bytes 5390468 | tf_op jit(solution)/shard_map/while/body/eval_jaxpr/hpn,hnt->hpt/dot_general | solution.py:44
  127.7 0.8 copy-done.9
  129.2 3.6 %convolution_add_fusion.2 = f32[32,16,256]{2,1,0:T(8,128)S(1)} fusion(f32[32,256,128]{2,1,0:T(8,128)S(1)} %bitcast.193, f32[32,16,256]{2,1,0:T(8,128)S(1)} %get-tuple-element.551, f32[32]{0:T(128)S(1)} %exp.74, f32[32,128]{1,0:T(8,128)S(1)} %get-tuple-element.520, bf16[4,32,16,128]{3,2,1,0:T(8,128)(2,1)S(1)} %get-tuple-element.566, ...), kind=kOutput, calls=%fused_computation.36.clone.1 | convolution fusion | flops 201719808 | bytes 5390852 | tf_op jit(solution)/shard_map/while/body/eval_jaxpr/hps,hns->hpn/dot_general | solution.py:50
  134.0 1.7 fusion.87
  137.7 3.1 %fusion.88 = bf16[4,32,16,128]{3,2,1,0:T(8,128)(2,1)S(1)} fusion(bf16[4,32,16,128]{3,2,1,0:T(8,128)(2,1)S(1)} %copy-done.8, s32[]{:T(128)} %get-tuple-element.550, f32[32,16,128]{2,1,0:T(8,128)S(1)} %fusion.87, f32[32,256,128]{2,1,0:T(8,128)S(1)} %bitcast.192, f32[32,16,256]{2,1,0:T(8,128)S(1)} %get-tuple-element.551, f32[32]{0:T(128)} %get-tuple-element.569, ...), kind=kOutput, calls=%fused_computation.42.clone.1 | convolution fusion | flops 201654272 | bytes 5390468 | tf_op jit(solution)/shard_map/while/body/eval_jaxpr/hpn,hnt->hpt/dot_general | solution.py:44
  140.8 0.8 copy-done.9
  142.2 3.6 %convolution_add_fusion.2 = f32[32,16,256]{2,1,0:T(8,128)S(1)} fusion(f32[32,256,128]{2,1,0:T(8,128)S(1)} %bitcast.193, f32[32,16,256]{2,1,0:T(8,128)S(1)} %get-tuple-element.551, f32[32]{0:T(128)S(1)} %exp.74, f32[32,128]{1,0:T(8,128)S(1)} %get-tuple-element.520, bf16[4,32,16,128]{3,2,1,0:T(8,128)(2,1)S(1)} %get-tuple-element.566, ...), kind=kOutput, calls=%fused_computation.36.clone.1 | convolution fusion | flops 201719808 | bytes 5390852 | tf_op jit(solution)/shard_map/while/body/eval_jaxpr/hps,hns->hpn/dot_general | solution.py:50
  147.1 1.7 fusion.87
  150.7 3.1 %fusion.88 = bf16[4,32,16,128]{3,2,1,0:T(8,128)(2,1)S(1)} fusion(bf16[4,32,16,128]{3,2,1,0:T(8,128)(2,1)S(1)} %copy-done.8, s32[]{:T(128)} %get-tuple-element.550, f32[32,16,128]{2,1,0:T(8,128)S(1)} %fusion.87, f32[32,256,128]{2,1,0:T(8,128)S(1)} %bitcast.192, f32[32,16,256]{2,1,0:T(8,128)S(1)} %get-tuple-element.551, f32[32]{0:T(128)} %get-tuple-element.569, ...), kind=kOutput, calls=%fused_computation.42.clone.1 | convolution fusion | flops 201654272 | bytes 5390468 | tf_op jit(solution)/shard_map/while/body/eval_jaxpr/hpn,hnt->hpt/dot_general | solution.py:44
  153.8 0.8 copy-done.9
  155.2 3.6 %convolution_add_fusion.2 = f32[32,16,256]{2,1,0:T(8,128)S(1)} fusion(f32[32,256,128]{2,1,0:T(8,128)S(1)} %bitcast.193, f32[32,16,256]{2,1,0:T(8,128)S(1)} %get-tuple-element.551, f32[32]{0:T(128)S(1)} %exp.74, f32[32,128]{1,0:T(8,128)S(1)} %get-tuple-element.520, bf16[4,32,16,128]{3,2,1,0:T(8,128)(2,1)S(1)} %get-tuple-element.566, ...), kind=kOutput, calls=%fused_computation.36.clone.1 | convolution fusion | flops 201719808 | bytes 5390852 | tf_op jit(solution)/shard_map/while/body/eval_jaxpr/hps,hns->hpn/dot_general | solution.py:50
  160.1 1.7 fusion.87
  163.8 3.1 %fusion.88 = bf16[4,32,16,128]{3,2,1,0:T(8,128)(2,1)S(1)} fusion(bf16[4,32,16,128]{3,2,1,0:T(8,128)(2,1)S(1)} %copy-done.8, s32[]{:T(128)} %get-tuple-element.550, f32[32,16,128]{2,1,0:T(8,128)S(1)} %fusion.87, f32[32,256,128]{2,1,0:T(8,128)S(1)} %bitcast.192, f32[32,16,256]{2,1,0:T(8,128)S(1)} %get-tuple-element.551, f32[32]{0:T(128)} %get-tuple-element.569, ...), kind=kOutput, calls=%fused_computation.42.clone.1 | convolution fusion | flops 201654272 | bytes 5390468 | tf_op jit(solution)/shard_map/while/body/eval_jaxpr/hpn,hnt->hpt/dot_general | solution.py:44
  166.9 0.8 copy-done.9
  168.3 3.6 %convolution_add_fusion.2 = f32[32,16,256]{2,1,0:T(8,128)S(1)} fusion(f32[32,256,128]{2,1,0:T(8,128)S(1)} %bitcast.193, f32[32,16,256]{2,1,0:T(8,128)S(1)} %get-tuple-element.551, f32[32]{0:T(128)S(1)} %exp.74, f32[32,128]{1,0:T(8,128)S(1)} %get-tuple-element.520, bf16[4,32,16,128]{3,2,1,0:T(8,128)(2,1)S(1)} %get-tuple-element.566, ...), kind=kOutput, calls=%fused_computation.36.clone.1 | convolution fusion | flops 201719808 | bytes 5390852 | tf_op jit(solution)/shard_map/while/body/eval_jaxpr/hps,hns->hpn/dot_general | solution.py:50
  171.9 1.6 copy.79
  173.8 1.6 select_convert_fusion.1
  175.4 7.0 %all-gather.2.cloned.1.call-done = bf16[2,4608,256]{2,1,0:T(8,128)(2,1)} async-done(((bf16[2,1152,256]{2,1,0:T(8,128)(2,1)}), bf16[2,4608,256]{2,1,0:T(8,128)(2,1)}) %all-gather.2.cloned.1.call-update) | async-done | bytes 4718608 | tf_op jit(solution)/shard_map/all_gather | solution.py:154
  182.4 94.4 %while.33 = (s32[]{:T(128)}, f32[128,2,8]{0,2,1:T(8,128)S(1)}, f32[128,2,8]{0,2,1:T(8,128)S(1)}, f32[128,2,8,128]{0,3,2,1:T(8,128)}, s32[4]{0:T(128)S(1)}, /*ind...) while((s32[]{:T(128)}, f32[128,2,8]{0,2,1:T(8,128)S(1)}, ...), condition=%wide.region_11.12_spmd.clone, body=%wide.region_8.11_spmd.clone.sunk | while | flops 1235016192 | bytes 47004440 | solution.py:165
  184.5 0.7 iota_compare_fusion.8
  185.2 1.1 compare_select_fusion.7
  186.2 1.3 constant_dynamic-slice_fusion.10
  188.0 5.3 %fusion.92 = (f32[128,2,8]{0,2,1:T(8,128)S(1)}, f32[2,1152,128,8]{2,1,3,0:T(8,128)}) fusion(pred[128,1152]{0,1:T(8,128)(4,1)S(1)} %compare_select_fusion.7, bf16[1152,2,128,1]{0,2,3,1:T(8,128)(2,1)S(1)} %bitcast.196, bf16[128,2,8,128]{3,2,1,0:T(8,128)(2,1)S(1)} %bitcast.194), kind=kOutput, calls=%fused_computation.9.clone.1 | convolution fusion | flops 611055616 | bytes 10706944 | tf_op jit(solution)/shard_map/while/body/eval_jaxpr/rgqd,kgd->rgqk/dot_general | solution.py:121
  193.3 5.6 %fusion.93 = f32[128,2,8]{0,2,1:T(8,128)S(1)} fusion(f32[2,1152,128,8]{2,1,3,0:T(8,128)} %get-tuple-element.535, f32[128,2,8]{0,2,1:T(8,128)S(1)} %select_maximum_fusion.2, pred[128,1152]{0,1:T(8,128)(4,1)S(1)} %compare_select_fusion.7), kind=kLoop, calls=%fused_computation.13.clone.1 | loop fusion | flops 9435136 | bytes 9601024 | tf_op jit(solution)/shard_map/while/body/eval_jaxpr/reduce_sum | solution.py:128
  199.2 5.9 %fusion.95 = f32[128,2,8,128]{0,3,2,1:T(8,128)S(1)} fusion(bf16[1152,2,128,1]{0,2,3,1:T(8,128)(2,1)S(1)} %bitcast.197, f32[2,1152,128,8]{2,1,3,0:T(8,128)} %get-tuple-element.535, f32[128,2,8]{0,2,1:T(8,128)S(1)} %select_maximum_fusion.2, pred[128,1152]{0,1:T(8,128)(4,1)S(1)} %compare_select_fusion.7, f32[128,2,8,128]{0,3,2,1:T(8,128)S(1)} %copy-done.3, ...), kind=kOutput, calls=%fused_computation.17.clone.1 | convolution fusion | flops 614203392 | bytes 12288001 | tf_op jit(solution)/shard_map/while/body/eval_jaxpr/rgqk,kgd->rgqd/dot_general | solution.py:129
  205.2 0.9 copy-done.4
  208.7 1.1 compare_select_fusion.7
  209.8 1.3 constant_dynamic-slice_fusion.10
  211.5 5.3 %fusion.92 = (f32[128,2,8]{0,2,1:T(8,128)S(1)}, f32[2,1152,128,8]{2,1,3,0:T(8,128)}) fusion(pred[128,1152]{0,1:T(8,128)(4,1)S(1)} %compare_select_fusion.7, bf16[1152,2,128,1]{0,2,3,1:T(8,128)(2,1)S(1)} %bitcast.196, bf16[128,2,8,128]{3,2,1,0:T(8,128)(2,1)S(1)} %bitcast.194), kind=kOutput, calls=%fused_computation.9.clone.1 | convolution fusion | flops 611055616 | bytes 10706944 | tf_op jit(solution)/shard_map/while/body/eval_jaxpr/rgqd,kgd->rgqk/dot_general | solution.py:121
  216.8 5.6 %fusion.93 = f32[128,2,8]{0,2,1:T(8,128)S(1)} fusion(f32[2,1152,128,8]{2,1,3,0:T(8,128)} %get-tuple-element.535, f32[128,2,8]{0,2,1:T(8,128)S(1)} %select_maximum_fusion.2, pred[128,1152]{0,1:T(8,128)(4,1)S(1)} %compare_select_fusion.7), kind=kLoop, calls=%fused_computation.13.clone.1 | loop fusion | flops 9435136 | bytes 9601024 | tf_op jit(solution)/shard_map/while/body/eval_jaxpr/reduce_sum | solution.py:128
  222.8 5.9 %fusion.95 = f32[128,2,8,128]{0,3,2,1:T(8,128)S(1)} fusion(bf16[1152,2,128,1]{0,2,3,1:T(8,128)(2,1)S(1)} %bitcast.197, f32[2,1152,128,8]{2,1,3,0:T(8,128)} %get-tuple-element.535, f32[128,2,8]{0,2,1:T(8,128)S(1)} %select_maximum_fusion.2, pred[128,1152]{0,1:T(8,128)(4,1)S(1)} %compare_select_fusion.7, f32[128,2,8,128]{0,3,2,1:T(8,128)S(1)} %copy-done.3, ...), kind=kOutput, calls=%fused_computation.17.clone.1 | convolution fusion | flops 614203392 | bytes 12288001 | tf_op jit(solution)/shard_map/while/body/eval_jaxpr/rgqk,kgd->rgqd/dot_general | solution.py:129
  228.7 0.9 copy-done.4
  231.5 0.7 iota_compare_fusion.8
  232.2 1.1 compare_select_fusion.7
  233.3 1.3 constant_dynamic-slice_fusion.10
  235.0 5.3 %fusion.92 = (f32[128,2,8]{0,2,1:T(8,128)S(1)}, f32[2,1152,128,8]{2,1,3,0:T(8,128)}) fusion(pred[128,1152]{0,1:T(8,128)(4,1)S(1)} %compare_select_fusion.7, bf16[1152,2,128,1]{0,2,3,1:T(8,128)(2,1)S(1)} %bitcast.196, bf16[128,2,8,128]{3,2,1,0:T(8,128)(2,1)S(1)} %bitcast.194), kind=kOutput, calls=%fused_computation.9.clone.1 | convolution fusion | flops 611055616 | bytes 10706944 | tf_op jit(solution)/shard_map/while/body/eval_jaxpr/rgqd,kgd->rgqk/dot_general | solution.py:121
  240.3 5.6 %fusion.93 = f32[128,2,8]{0,2,1:T(8,128)S(1)} fusion(f32[2,1152,128,8]{2,1,3,0:T(8,128)} %get-tuple-element.535, f32[128,2,8]{0,2,1:T(8,128)S(1)} %select_maximum_fusion.2, pred[128,1152]{0,1:T(8,128)(4,1)S(1)} %compare_select_fusion.7), kind=kLoop, calls=%fused_computation.13.clone.1 | loop fusion | flops 9435136 | bytes 9601024 | tf_op jit(solution)/shard_map/while/body/eval_jaxpr/reduce_sum | solution.py:128
  246.3 5.9 %fusion.95 = f32[128,2,8,128]{0,3,2,1:T(8,128)S(1)} fusion(bf16[1152,2,128,1]{0,2,3,1:T(8,128)(2,1)S(1)} %bitcast.197, f32[2,1152,128,8]{2,1,3,0:T(8,128)} %get-tuple-element.535, f32[128,2,8]{0,2,1:T(8,128)S(1)} %select_maximum_fusion.2, pred[128,1152]{0,1:T(8,128)(4,1)S(1)} %compare_select_fusion.7, f32[128,2,8,128]{0,3,2,1:T(8,128)S(1)} %copy-done.3, ...), kind=kOutput, calls=%fused_computation.17.clone.1 | convolution fusion | flops 614203392 | bytes 12288001 | tf_op jit(solution)/shard_map/while/body/eval_jaxpr/rgqk,kgd->rgqd/dot_general | solution.py:129
  252.2 0.9 copy-done.4
  255.1 0.7 iota_compare_fusion.8
  255.8 1.1 compare_select_fusion.7
  256.8 1.3 constant_dynamic-slice_fusion.10
  258.6 5.3 %fusion.92 = (f32[128,2,8]{0,2,1:T(8,128)S(1)}, f32[2,1152,128,8]{2,1,3,0:T(8,128)}) fusion(pred[128,1152]{0,1:T(8,128)(4,1)S(1)} %compare_select_fusion.7, bf16[1152,2,128,1]{0,2,3,1:T(8,128)(2,1)S(1)} %bitcast.196, bf16[128,2,8,128]{3,2,1,0:T(8,128)(2,1)S(1)} %bitcast.194), kind=kOutput, calls=%fused_computation.9.clone.1 | convolution fusion | flops 611055616 | bytes 10706944 | tf_op jit(solution)/shard_map/while/body/eval_jaxpr/rgqd,kgd->rgqk/dot_general | solution.py:121
  263.9 5.6 %fusion.93 = f32[128,2,8]{0,2,1:T(8,128)S(1)} fusion(f32[2,1152,128,8]{2,1,3,0:T(8,128)} %get-tuple-element.535, f32[128,2,8]{0,2,1:T(8,128)S(1)} %select_maximum_fusion.2, pred[128,1152]{0,1:T(8,128)(4,1)S(1)} %compare_select_fusion.7), kind=kLoop, calls=%fused_computation.13.clone.1 | loop fusion | flops 9435136 | bytes 9601024 | tf_op jit(solution)/shard_map/while/body/eval_jaxpr/reduce_sum | solution.py:128
  269.8 5.9 %fusion.95 = f32[128,2,8,128]{0,3,2,1:T(8,128)S(1)} fusion(bf16[1152,2,128,1]{0,2,3,1:T(8,128)(2,1)S(1)} %bitcast.197, f32[2,1152,128,8]{2,1,3,0:T(8,128)} %get-tuple-element.535, f32[128,2,8]{0,2,1:T(8,128)S(1)} %select_maximum_fusion.2, pred[128,1152]{0,1:T(8,128)(4,1)S(1)} %compare_select_fusion.7, f32[128,2,8,128]{0,3,2,1:T(8,128)S(1)} %copy-done.3, ...), kind=kOutput, calls=%fused_computation.17.clone.1 | convolution fusion | flops 614203392 | bytes 12288001 | tf_op jit(solution)/shard_map/while/body/eval_jaxpr/rgqk,kgd->rgqd/dot_general | solution.py:129
  275.8 0.9 copy-done.4
  276.7 1.3 broadcast_divide_fusion
  278.3 1.0 select_convert_fusion
  (214 shorter events, 24.7 us)
Async XLA Ops:
  7.2 26.5 %copy-start.2 = (bf16[1,32,2,32,256]{4,3,2,1,0:T(8,128)(2,1)S(1)}, bf16[1,32,2,32,256]{4,3,2,1,0:T(8,128)(2,1)}, u32[]{:S(2)}) copy-start(bf16[1,32,2,32,256]{4,3,2,1,0:T(8,128)(2,1)} %param.18) | copy-start | bytes 3145732
  15.6 32.8 %all-to-all-start = ((bf16[32,2,16,256]{3,2,1,0:T(8,128)(2,1)}), bf16[32,2,16,256]{3,2,1,0:T(8,128)(2,1)S(1)}, u32[]{:S(2)}, u32[]{:S(2)}) async-start(bf16[32,2,16,256]{3,2,1,0:T(8,128)(2,1)} %scatter_fusion), calls=%async_computation | async-start | bytes 1048576 | tf_op jit(solution)/shard_map/all_to_all | solution.py:88
  33.7 23.7 %copy-start.11 = (f32[1,32,512]{2,1,0:T(8,128)S(1)}, f32[1,32,512]{2,1,0:T(8,128)}, u32[]{:S(2)}) copy-start(f32[1,32,512]{2,1,0:T(8,128)} %param.27) | copy-start | bytes 196612
  33.7 23.7 %copy-start.5 = (bf16[1,32,16,512]{3,2,1,0:T(8,128)(2,1)S(1)}, bf16[1,32,16,512]{3,2,1,0:T(8,128)(2,1)}, u32[]{:S(2)}) copy-start(bf16[1,32,16,512]{3,2,1,0:T(8,128)(2,1)} %param.24) | copy-start | bytes 1572868
  33.7 24.0 %copy-start.6 = (bf16[1,2,256,512]{3,2,1,0:T(8,128)(2,1)S(1)}, bf16[1,2,256,512]{3,2,1,0:T(8,128)(2,1)}, u32[]{:S(2)}) copy-start(bf16[1,2,256,512]{3,2,1,0:T(8,128)(2,1)} %param.25) | copy-start | bytes 1572868
  38.7 19.2 %copy-start.7 = (bf16[1,2,256,512]{3,2,1,0:T(8,128)(2,1)S(1)}, bf16[1,2,256,512]{3,2,1,0:T(8,128)(2,1)}, u32[]{:S(2)}) copy-start(bf16[1,2,256,512]{3,2,1,0:T(8,128)(2,1)} %param.26) | copy-start | bytes 1572868
  38.7 19.4 %copy-start.14 = (s32[1,1024]{1,0:T(1,128)S(1)}, s32[1,1024]{1,0:T(1,128)}, u32[]{:S(2)}) copy-start(s32[1,1024]{1,0:T(1,128)} %param.20) | copy-start | bytes 12292
  38.7 19.4 %copy-start.17 = (s32[1,1024]{1,0:T(1,128)S(1)}, s32[1,1024]{1,0:T(1,128)}, u32[]{:S(2)}) copy-start(s32[1,1024]{1,0:T(1,128)} %param.21) | copy-start | bytes 12292
  38.7 25.1 %copy-start.19 = (f32[32]{0:T(128)S(1)}, f32[32]{0:T(128)}, u32[]{:S(2)}) copy-start(f32[32]{0:T(128)} %param.28) | copy-start | bytes 388
  48.4 65.7 %all-to-all-start.1 = ((bf16[32,2,2,32,256]{4,3,2,1,0:T(8,128)(2,1)}), bf16[32,2,2,32,256]{4,3,2,1,0:T(8,128)(2,1)}, u32[]{:S(2)}, u32[]{:S(2)}) async-start(bf16[32,2,2,32,256]{4,3,2,1,0:T(8,128)(2,1)} %scatter_fusion.1), calls=%async_computation.1 | async-start | bytes 4194304 | tf_op jit(solution)/shard_map/all_to_all | solution.py:87
  56.5 125.9 %all-gather.2.cloned.1.call-start = ((), (), s32[]{:S(2)}) async-start(), calls=%async_computation.2 | async-start | bytes 5898240 | tf_op jit(solution)/shard_map/all_gather | solution.py:154
  57.6 61.0 %copy-start.10 = (bf16[1,2,128,256]{3,2,1,0:T(8,128)(2,1)S(1)}, bf16[1,2,128,256]{3,2,1,0:T(8,128)(2,1)}, u32[]{:S(2)}) copy-start(bf16[1,2,128,256]{3,2,1,0:T(8,128)(2,1)} %param.31) | copy-start | bytes 393220
  119.7 62.6 %copy-start.1 = (bf16[1,128,2048]{2,1,0:T(8,128)(2,1)S(1)}, bf16[1,128,2048]{2,1,0:T(8,128)(2,1)}, u32[]{:S(2)}) copy-start(bf16[1,128,2048]{2,1,0:T(8,128)(2,1)} %param.30) | copy-start | bytes 1572868
  119.8 3.3 %copy-start.15 = (f32[32,1]{0,1:T(1,128)}, f32[32,1]{0,1:T(1,128)S(1)}, u32[]{:S(2)}) copy-start(f32[32,1]{0,1:T(1,128)S(1)} %get-tuple-element.564) | copy-start | bytes 388 | tf_op jit(solution)/shard_map/while
  122.9 0.5 copy-start.12
  123.6 1.0 copy-start.8
  123.6 4.1 %copy-start.13 = (f32[32]{0:T(128)S(1)}, f32[32]{0:T(128)}, u32[]{:S(2)}) copy-start(f32[32]{0:T(128)} %copy-done.12) | copy-start | bytes 388 | tf_op jit(solution)/shard_map/while
  127.7 0.8 copy-start.9
  128.7 4.1 %copy-start.16 = (f32[32,1]{0,1:T(1,128)S(1)}, f32[32,1]{0,1:T(1,128)}, u32[]{:S(2)}) copy-start(f32[32,1]{0,1:T(1,128)} %copy-done.15) | copy-start | bytes 388 | tf_op jit(solution)/shard_map/while
  132.8 3.2 %copy-start.15 = (f32[32,1]{0,1:T(1,128)}, f32[32,1]{0,1:T(1,128)S(1)}, u32[]{:S(2)}) copy-start(f32[32,1]{0,1:T(1,128)S(1)} %get-tuple-element.564) | copy-start | bytes 388 | tf_op jit(solution)/shard_map/while
  136.0 0.5 copy-start.12
  136.6 1.0 copy-start.8
  136.6 4.1 %copy-start.13 = (f32[32]{0:T(128)S(1)}, f32[32]{0:T(128)}, u32[]{:S(2)}) copy-start(f32[32]{0:T(128)} %copy-done.12) | copy-start | bytes 388 | tf_op jit(solution)/shard_map/while
  140.8 0.8 copy-start.9
  141.7 4.1 %copy-start.16 = (f32[32,1]{0,1:T(1,128)S(1)}, f32[32,1]{0,1:T(1,128)}, u32[]{:S(2)}) copy-start(f32[32,1]{0,1:T(1,128)} %copy-done.15) | copy-start | bytes 388 | tf_op jit(solution)/shard_map/while
  145.8 3.3 %copy-start.15 = (f32[32,1]{0,1:T(1,128)}, f32[32,1]{0,1:T(1,128)S(1)}, u32[]{:S(2)}) copy-start(f32[32,1]{0,1:T(1,128)S(1)} %get-tuple-element.564) | copy-start | bytes 388 | tf_op jit(solution)/shard_map/while
  149.0 0.5 copy-start.12
  149.7 1.0 copy-start.8
  149.7 4.1 %copy-start.13 = (f32[32]{0:T(128)S(1)}, f32[32]{0:T(128)}, u32[]{:S(2)}) copy-start(f32[32]{0:T(128)} %copy-done.12) | copy-start | bytes 388 | tf_op jit(solution)/shard_map/while
  153.8 0.8 copy-start.9
  154.8 4.1 %copy-start.16 = (f32[32,1]{0,1:T(1,128)S(1)}, f32[32,1]{0,1:T(1,128)}, u32[]{:S(2)}) copy-start(f32[32,1]{0,1:T(1,128)} %copy-done.15) | copy-start | bytes 388 | tf_op jit(solution)/shard_map/while
  158.9 3.3 %copy-start.15 = (f32[32,1]{0,1:T(1,128)}, f32[32,1]{0,1:T(1,128)S(1)}, u32[]{:S(2)}) copy-start(f32[32,1]{0,1:T(1,128)S(1)} %get-tuple-element.564) | copy-start | bytes 388 | tf_op jit(solution)/shard_map/while
  162.0 0.5 copy-start.12
  162.7 1.0 copy-start.8
  162.7 4.1 %copy-start.13 = (f32[32]{0:T(128)S(1)}, f32[32]{0:T(128)}, u32[]{:S(2)}) copy-start(f32[32]{0:T(128)} %copy-done.12) | copy-start | bytes 388 | tf_op jit(solution)/shard_map/while
  166.8 0.8 copy-start.9
  167.8 4.1 %copy-start.16 = (f32[32,1]{0,1:T(1,128)S(1)}, f32[32,1]{0,1:T(1,128)}, u32[]{:S(2)}) copy-start(f32[32,1]{0,1:T(1,128)} %copy-done.15) | copy-start | bytes 388 | tf_op jit(solution)/shard_map/while
  171.9 10.5 %copy-start = (f32[32,16,256]{2,1,0:T(8,128)}, f32[32,16,256]{2,1,0:T(8,128)S(1)}, u32[]{:S(2)}) copy-start(f32[32,16,256]{2,1,0:T(8,128)S(1)} %get-tuple-element.235) | copy-start | bytes 1572868
  182.4 95.9 %copy-start.18 = (pred[128]{0:T(512)(128)(4,1)S(1)}, pred[128]{0:T(512)(128)(4,1)}, u32[]{:S(2)}) copy-start(pred[128]{0:T(512)(128)(4,1)} %add_compare_fusion.1) | copy-start | bytes 388
  193.3 6.0 %copy-start.3 = (f32[128,2,8,128]{0,3,2,1:T(8,128)S(1)}, f32[128,2,8,128]{0,3,2,1:T(8,128)}, u32[]{:S(2)}) copy-start(f32[128,2,8,128]{0,3,2,1:T(8,128)} %get-tuple-element.589) | copy-start | bytes 3145732 | tf_op jit(solution)/shard_map/while
  205.2 1.0 copy-start.4
  216.8 6.0 %copy-start.3 = (f32[128,2,8,128]{0,3,2,1:T(8,128)S(1)}, f32[128,2,8,128]{0,3,2,1:T(8,128)}, u32[]{:S(2)}) copy-start(f32[128,2,8,128]{0,3,2,1:T(8,128)} %get-tuple-element.589) | copy-start | bytes 3145732 | tf_op jit(solution)/shard_map/while
  228.7 1.0 copy-start.4
  240.3 6.0 %copy-start.3 = (f32[128,2,8,128]{0,3,2,1:T(8,128)S(1)}, f32[128,2,8,128]{0,3,2,1:T(8,128)}, u32[]{:S(2)}) copy-start(f32[128,2,8,128]{0,3,2,1:T(8,128)} %get-tuple-element.589) | copy-start | bytes 3145732 | tf_op jit(solution)/shard_map/while
  252.2 1.0 copy-start.4
  263.8 6.0 %copy-start.3 = (f32[128,2,8,128]{0,3,2,1:T(8,128)S(1)}, f32[128,2,8,128]{0,3,2,1:T(8,128)}, u32[]{:S(2)}) copy-start(f32[128,2,8,128]{0,3,2,1:T(8,128)} %get-tuple-element.589) | copy-start | bytes 3145732 | tf_op jit(solution)/shard_map/while
  275.7 1.0 copy-start.4
Sparse Core Ops, SparseCore 0:
  119.8 62.4 all-gather.1
where the time goes:
time: 287 us; the launch traced here: 286 us
  matrix products  79.2 us (28%)
  waiting for transfers between devices  66.3 us (23%)
  local copies, waits for them, and re-layouts  51.9 us (18%)
  other arithmetic  42.7 us (15%)
  starting transfers between devices  24.6 us (9%)
  between operations  15 us (5%)
  loops' own time  6.46 us (2%)
    all_to_all x1, waiting for transfers between devices, route_blocks(): lax.all_to_all(send_kv, 'pool', split_axis=0, concat_axis=0, tiled=True)  49.6 us
    dot_general x4, matrix products, attend_block(): jnp.einsum('rgqk,kgd->rgqd', weights.astype(jnp.bfloat16), value_heads, p...  23.6 us
    reduce_sum x4, other arithmetic, attend_block(): totals = fade * totals + jnp.sum(weights, axis=-1)  22.6 us
    dot_general x4, matrix products, attend_block(): jnp.einsum('rgqd,kgd->rgqk', query_heads, key_heads, preferred_element_ty...  21.1 us
    all_to_all x1, starting transfers between devices, route_blocks(): lax.all_to_all(send_state, 'pool', split_axis=0, concat_axis=0, tiled=True)  16.5 us
    dot_general x4, matrix products, advance(): jnp.einsum('hps,hns->hpn', value_blk * weights[:, None, :], write_in, pre...  14.5 us
    while x80, local copies, waits for them, and re-layouts  13.7 us
    dot_general x4, matrix products, advance(): jnp.einsum('hpn,hnt->hpt', carried, read_out, precision=exact)  12.3 us
  transfers between devices with their start and end apart: 3, of which 3 were waited for; matrix products, arithmetic and copies ran while one was open for 21% of the time, Pallas kernels for 0%

commit v1 on v0

--- a/solution.py
+++ b/solution.py
@@ -151,7 +151,9 @@
         jnp.zeros((turn_rows, groups, per_group), jnp.float32),
         jnp.zeros((turn_rows, groups, per_group, HEAD_DIM), jnp.float32),
     )
-    piece = lax.all_gather(local_keys, "ctx", axis=1, tiled=True)
+    piece = jnp.concatenate(
+        lax.all_to_all(jnp.stack([local_keys] * lax.axis_size("ctx")), "ctx", 0, 0), axis=1
+    )
     count = piece.shape[1] // seg_rows
     blocks = piece.reshape(2, count, seg_rows, width).transpose(1, 0, 2, 3)
 

time: 287 us -> 266 us (0.927)
  the two profiles are of different devices: /device:TPU:1 before, /device:TPU:160 now
where the time goes in v1:
time: 266 us; the launch traced here: 265 us
  waiting for transfers between devices  69.9 us (26%)
  matrix products  68.7 us (26%)
  local copies, waits for them, and re-layouts  49.6 us (19%)
  other arithmetic  40.1 us (15%)
  starting transfers between devices  28.7 us (11%)
  loops' own time  6.12 us (2%)
    all_to_all x1, waiting for transfers between devices, route_blocks(): lax.all_to_all(send_kv, 'pool', split_axis=0, concat_axis=0, tiled=True)  57 us
    reduce_sum x4, other arithmetic, attend_block(): totals = fade * totals + jnp.sum(weights, axis=-1)  22.8 us
    dot_general x4, matrix products, attend_block(): jnp.einsum('rgqd,kgd->rgqk', query_heads, key_heads, preferred_element_ty...  21.1 us
    dot_general x4, matrix products, attend_block(): jnp.einsum('rgqk,kgd->rgqd', weights.astype(jnp.bfloat16), value_heads, p...  15.8 us
    dot_general x4, matrix products, advance(): jnp.einsum('hps,hns->hpn', value_blk * weights[:, None, :], write_in, pre...  14.5 us
    all_to_all x1, starting transfers between devices, route_blocks(): lax.all_to_all(send_state, 'pool', split_axis=0, concat_axis=0, tiled=True)  14 us
    dot_general x4, matrix products, advance(): jnp.einsum('hpn,hnt->hpt', carried, read_out, precision=exact)  9.66 us
    all_to_all x1, starting transfers between devices, route_blocks(): lax.all_to_all(send_kv, 'pool', split_axis=0, concat_axis=0, tiled=True)  9.46 us
  transfers between devices with their start and end apart: 3, of which 3 were waited for; matrix products, arithmetic and copies ran while one was open for 21% of the time, Pallas kernels for 0%

profile of v1, /device:TPU:160, one launch (start us, length us, event | category | flops | bytes accessed | tf_op | source)
XLA Modules:
  0.0 264.8 jit_solution(3307555441109738215)
XLA Ops:
  1.2 1.3 reduce.7
  2.7 1.0 fusion.51
  3.9 0.9 broadcast_in_dim.176
  4.8 4.3 %scatter_fusion = bf16[32,2,16,256]{3,2,1,0:T(8,128)(2,1)} fusion(bf16[32,2,16,256]{3,2,1,0:T(8,128)(2,1)} %broadcast_in_dim.176, s32[32]{0:T(128)S(1)} %fusion.47, bf16[32,16,256]{2,1,0:T(8,128)(2,1)} %param.19), kind=kCustom, calls=%fused_computation.2 | custom fusion | bytes 786688 | tf_op jit(solution)/shard_map/scatter | solution.py:84
  9.1 14.0 %all-to-all-start = ((bf16[32,2,16,256]{3,2,1,0:T(8,128)(2,1)}), bf16[32,2,16,256]{3,2,1,0:T(8,128)(2,1)S(1)}, u32[]{:S(2)}, u32[]{:S(2)}) async-start(bf16[32,2,16,256]{3,2,1,0:T(8,128)(2,1)} %scatter_fusion), calls=%async_computation | async-start | bytes 1048576 | tf_op jit(solution)/shard_map/all_to_all | solution.py:88
  23.1 1.6 broadcast_in_dim.189
  24.7 4.9 %scatter_fusion.1 = bf16[32,2,2,32,256]{4,3,2,1,0:T(8,128)(2,1)} fusion(bf16[32,2,2,32,256]{4,3,2,1,0:T(8,128)(2,1)} %broadcast_in_dim.189, s32[32]{0:T(128)S(1)} %fusion.47, bf16[32,2,32,256]{3,2,1,0:T(8,128)(2,1)S(1)} %bitcast.206), kind=kCustom, calls=%fused_computation.4 | custom fusion | bytes 3145984 | tf_op jit(solution)/shard_map/scatter | solution.py:79
  29.6 8.7 %all-to-all-done = bf16[32,2,16,256]{3,2,1,0:T(8,128)(2,1)S(1)} async-done(((bf16[32,2,16,256]{3,2,1,0:T(8,128)(2,1)}), bf16[32,2,16,256]{3,2,1,0:T(8,128)(2,1)S(1)}, u32[]{:S(2)}, u32[]{:S(2)}) %all-to-all-start) | async-done | bytes 524320 | tf_op jit(solution)/shard_map/all_to_all | solution.py:88
  38.3 9.5 %all-to-all-start.1 = ((bf16[32,2,2,32,256]{4,3,2,1,0:T(8,128)(2,1)}), bf16[32,2,2,32,256]{4,3,2,1,0:T(8,128)(2,1)}, u32[]{:S(2)}, u32[]{:S(2)}) async-start(bf16[32,2,2,32,256]{4,3,2,1,0:T(8,128)(2,1)} %scatter_fusion.1), calls=%async_computation.1 | async-start | bytes 4194304 | tf_op jit(solution)/shard_map/all_to_all | solution.py:87
  49.4 4.3 %scatter_custom_fusion.1 = s32[32]{0:T(128)S(1)} fusion(s32[1024]{0:T(1024)S(1)} %bitcast.210, s32[1024]{0:T(1024)S(1)} %reshape.367, s32[]{:T(128)} %constant.117.clone.1), kind=kCustom, calls=%fused_computation.95 | custom fusion | bytes 132 | tf_op jit(solution)/shard_map/scatter | solution.py:92
  54.4 57.0 %all-to-all-done.1 = bf16[32,2,2,32,256]{4,3,2,1,0:T(8,128)(2,1)} async-done(((bf16[32,2,2,32,256]{4,3,2,1,0:T(8,128)(2,1)}), bf16[32,2,2,32,256]{4,3,2,1,0:T(8,128)(2,1)}, u32[]{:S(2)}, u32[]{:S(2)}) %all-to-all-start.1) | async-done | bytes 2097184 | tf_op jit(solution)/shard_map/all_to_all | solution.py:87
  111.5 2.2 gather_fusion.1
  113.9 1.4 copy.68
  115.3 4.0 %stack.2 = bf16[4,2,1152,256]{2,3,1,0:T(8,128)(2,1)} broadcast(bf16[2,1152,256]{1,2,0:T(8,128)(2,1)} %copy.68), dimensions={1,2,3} | broadcast | bytes 5898240 | tf_op jit(solution)/shard_map/stack | solution.py:155
  119.3 5.2 %all-to-all-start.2 = ((bf16[4,2,1152,256]{2,3,1,0:T(8,128)(2,1)}), bf16[4,2,1152,256]{2,3,1,0:T(8,128)(2,1)}, u32[]{:S(2)}, u32[]{:S(2)}) async-start(bf16[4,2,1152,256]{2,3,1,0:T(8,128)(2,1)} %stack.2), calls=%async_computation.2 | async-start | bytes 9437184 | tf_op jit(solution)/shard_map/all_to_all | solution.py:155
  124.6 47.7 %while.32 = (s32[]{:T(128)}, f32[32,16,256]{2,1,0:T(8,128)S(1)}, bf16[4,32,16,128]{3,2,1,0:T(8,128)(2,1)}, f32[32,1]{0,1:T(1,128)S(1)}, f32[4,32,128]{2,0,1:T(4,...) while((s32[]{:T(128)}, f32[32,16,256]{2,1,0:T(8,128)S(1)}, ...), condition=%wide.region_6.7_spmd.clone, body=%wide.region_4.6_spmd.clone.sunk | while | flops 524115968 | bytes 31067072 | solution.py:55
  125.8 1.7 fusion.87
  129.0 2.4 fusion.88
  131.5 0.8 copy-done.8
  132.9 3.6 %convolution_add_fusion.2 = f32[32,16,256]{2,1,0:T(8,128)S(1)} fusion(f32[32,256,128]{2,1,0:T(8,128)S(1)} %bitcast.190, f32[32,16,256]{2,1,0:T(8,128)S(1)} %get-tuple-element.506, f32[32]{0:T(128)S(1)} %exp.74, f32[32,128]{1,0:T(8,128)S(1)} %get-tuple-element.475, bf16[4,32,16,128]{3,2,1,0:T(8,128)(2,1)S(1)} %get-tuple-element.521, ...), kind=kOutput, calls=%fused_computation.36.clone.1 | convolution fusion | flops 201719808 | bytes 5390852 | tf_op jit(solution)/shard_map/while/body/eval_jaxpr/hps,hns->hpn/dot_general | solution.py:50
  137.7 1.7 fusion.87
  140.9 2.4 fusion.88
  143.4 0.8 copy-done.8
  144.8 3.6 %convolution_add_fusion.2 = f32[32,16,256]{2,1,0:T(8,128)S(1)} fusion(f32[32,256,128]{2,1,0:T(8,128)S(1)} %bitcast.190, f32[32,16,256]{2,1,0:T(8,128)S(1)} %get-tuple-element.506, f32[32]{0:T(128)S(1)} %exp.74, f32[32,128]{1,0:T(8,128)S(1)} %get-tuple-element.475, bf16[4,32,16,128]{3,2,1,0:T(8,128)(2,1)S(1)} %get-tuple-element.521, ...), kind=kOutput, calls=%fused_computation.36.clone.1 | convolution fusion | flops 201719808 | bytes 5390852 | tf_op jit(solution)/shard_map/while/body/eval_jaxpr/hps,hns->hpn/dot_general | solution.py:50
  149.6 1.7 fusion.87
  152.9 2.4 fusion.88
  155.3 0.8 copy-done.8
  156.7 3.6 %convolution_add_fusion.2 = f32[32,16,256]{2,1,0:T(8,128)S(1)} fusion(f32[32,256,128]{2,1,0:T(8,128)S(1)} %bitcast.190, f32[32,16,256]{2,1,0:T(8,128)S(1)} %get-tuple-element.506, f32[32]{0:T(128)S(1)} %exp.74, f32[32,128]{1,0:T(8,128)S(1)} %get-tuple-element.475, bf16[4,32,16,128]{3,2,1,0:T(8,128)(2,1)S(1)} %get-tuple-element.521, ...), kind=kOutput, calls=%fused_computation.36.clone.1 | convolution fusion | flops 201719808 | bytes 5390852 | tf_op jit(solution)/shard_map/while/body/eval_jaxpr/hps,hns->hpn/dot_general | solution.py:50
  161.6 1.7 fusion.87
  164.8 2.4 fusion.88
  167.2 0.8 copy-done.8
  168.6 3.6 %convolution_add_fusion.2 = f32[32,16,256]{2,1,0:T(8,128)S(1)} fusion(f32[32,256,128]{2,1,0:T(8,128)S(1)} %bitcast.190, f32[32,16,256]{2,1,0:T(8,128)S(1)} %get-tuple-element.506, f32[32]{0:T(128)S(1)} %exp.74, f32[32,128]{1,0:T(8,128)S(1)} %get-tuple-element.475, bf16[4,32,16,128]{3,2,1,0:T(8,128)(2,1)S(1)} %get-tuple-element.521, ...), kind=kOutput, calls=%fused_computation.36.clone.1 | convolution fusion | flops 201719808 | bytes 5390852 | tf_op jit(solution)/shard_map/while/body/eval_jaxpr/hps,hns->hpn/dot_general | solution.py:50
  172.3 1.6 copy.66
  174.1 0.9 select_convert_fusion.1
  175.0 4.2 %all-to-all-done.2 = bf16[4,2,1152,256]{2,3,1,0:T(8,128)(2,1)} async-done(((bf16[4,2,1152,256]{2,3,1,0:T(8,128)(2,1)}), bf16[4,2,1152,256]{2,3,1,0:T(8,128)(2,1)}, u32[]{:S(2)}, u32[]{:S(2)}) %all-to-all-start.2) | async-done | bytes 4718624 | tf_op jit(solution)/shard_map/all_to_all | solution.py:155
  179.2 83.0 %while.33 = (s32[]{:T(128)}, f32[128,2,8]{0,2,1:T(8,128)S(1)}, f32[128,2,8]{0,2,1:T(8,128)S(1)}, f32[128,2,8,128]{0,3,2,1:T(8,128)}, s32[4]{0:T(128)S(1)}, /*ind...) while((s32[]{:T(128)}, f32[128,2,8]{0,2,1:T(8,128)S(1)}, ...), condition=%wide.region_11.12_spmd.clone, body=%wide.region_8.11_spmd.clone.sunk | while | flops 1235016192 | bytes 74005248 | solution.py:167
  181.3 0.7 iota_compare_fusion.8
  182.0 1.1 compare_select_fusion.7
  183.1 1.3 constant_dynamic-slice_fusion.10
  184.6 5.3 %fusion.92 = (f32[128,2,8]{0,2,1:T(8,128)S(1)}, f32[2,1152,128,8]{2,1,3,0:T(8,128)}) fusion(pred[128,1152]{0,1:T(8,128)(4,1)S(1)} %compare_select_fusion.7, bf16[1152,2,128,1]{0,2,3,1:T(8,128)(2,1)S(1)} %bitcast.193, bf16[128,2,8,128]{3,2,1,0:T(8,128)(2,1)S(1)} %bitcast.191), kind=kOutput, calls=%fused_computation.9.clone.1 | convolution fusion | flops 611055616 | bytes 10706944 | tf_op jit(solution)/shard_map/while/body/eval_jaxpr/rgqd,kgd->rgqk/dot_general | solution.py:121
  189.8 5.7 %fusion.93 = f32[128,2,8]{0,2,1:T(8,128)S(1)} fusion(f32[2,1152,128,8]{2,1,3,0:T(8,128)} %get-tuple-element.490, f32[128,2,8]{0,2,1:T(8,128)S(1)} %select_maximum_fusion.2, pred[128,1152]{0,1:T(8,128)(4,1)S(1)} %compare_select_fusion.7), kind=kLoop, calls=%fused_computation.13.clone.1 | loop fusion | flops 9435136 | bytes 9601024 | tf_op jit(solution)/shard_map/while/body/eval_jaxpr/reduce_sum | solution.py:128
  195.6 0.6 copy-done
  196.2 3.0 %fusion.95 = f32[128,2,8,128]{0,3,2,1:T(8,128)} fusion(bf16[1152,2,128,1]{0,2,3,1:T(8,128)(2,1)S(1)} %bitcast.194, f32[2,1152,128,8]{2,1,3,0:T(8,128)S(1)} %copy-done, f32[128,2,8]{0,2,1:T(8,128)S(1)} %select_maximum_fusion.2, pred[128,1152]{0,1:T(8,128)(4,1)S(1)} %compare_select_fusion.7, f32[128,2,8,128]{0,3,2,1:T(8,128)} %get-tuple-element.544, ...), kind=kOutput, calls=%fused_computation.17.clone.1 | convolution fusion | flops 614203392 | bytes 12288001 | tf_op jit(solution)/shard_map/while/body/eval_jaxpr/rgqk,kgd->rgqd/dot_general | solution.py:129
  201.1 0.7 iota_compare_fusion.8
  201.8 1.1 compare_select_fusion.7
  202.9 1.3 constant_dynamic-slice_fusion.10
  204.3 5.3 %fusion.92 = (f32[128,2,8]{0,2,1:T(8,128)S(1)}, f32[2,1152,128,8]{2,1,3,0:T(8,128)}) fusion(pred[128,1152]{0,1:T(8,128)(4,1)S(1)} %compare_select_fusion.7, bf16[1152,2,128,1]{0,2,3,1:T(8,128)(2,1)S(1)} %bitcast.193, bf16[128,2,8,128]{3,2,1,0:T(8,128)(2,1)S(1)} %bitcast.191), kind=kOutput, calls=%fused_computation.9.clone.1 | convolution fusion | flops 611055616 | bytes 10706944 | tf_op jit(solution)/shard_map/while/body/eval_jaxpr/rgqd,kgd->rgqk/dot_general | solution.py:121
  209.6 5.7 %fusion.93 = f32[128,2,8]{0,2,1:T(8,128)S(1)} fusion(f32[2,1152,128,8]{2,1,3,0:T(8,128)} %get-tuple-element.490, f32[128,2,8]{0,2,1:T(8,128)S(1)} %select_maximum_fusion.2, pred[128,1152]{0,1:T(8,128)(4,1)S(1)} %compare_select_fusion.7), kind=kLoop, calls=%fused_computation.13.clone.1 | loop fusion | flops 9435136 | bytes 9601024 | tf_op jit(solution)/shard_map/while/body/eval_jaxpr/reduce_sum | solution.py:128
  215.3 0.6 copy-done
  216.0 4.3 %fusion.95 = f32[128,2,8,128]{0,3,2,1:T(8,128)} fusion(bf16[1152,2,128,1]{0,2,3,1:T(8,128)(2,1)S(1)} %bitcast.194, f32[2,1152,128,8]{2,1,3,0:T(8,128)S(1)} %copy-done, f32[128,2,8]{0,2,1:T(8,128)S(1)} %select_maximum_fusion.2, pred[128,1152]{0,1:T(8,128)(4,1)S(1)} %compare_select_fusion.7, f32[128,2,8,128]{0,3,2,1:T(8,128)} %get-tuple-element.544, ...), kind=kOutput, calls=%fused_computation.17.clone.1 | convolution fusion | flops 614203392 | bytes 12288001 | tf_op jit(solution)/shard_map/while/body/eval_jaxpr/rgqk,kgd->rgqd/dot_general | solution.py:129
  222.1 0.7 iota_compare_fusion.8
  222.8 1.1 compare_select_fusion.7
  223.9 1.3 constant_dynamic-slice_fusion.10
  225.3 5.3 %fusion.92 = (f32[128,2,8]{0,2,1:T(8,128)S(1)}, f32[2,1152,128,8]{2,1,3,0:T(8,128)}) fusion(pred[128,1152]{0,1:T(8,128)(4,1)S(1)} %compare_select_fusion.7, bf16[1152,2,128,1]{0,2,3,1:T(8,128)(2,1)S(1)} %bitcast.193, bf16[128,2,8,128]{3,2,1,0:T(8,128)(2,1)S(1)} %bitcast.191), kind=kOutput, calls=%fused_computation.9.clone.1 | convolution fusion | flops 611055616 | bytes 10706944 | tf_op jit(solution)/shard_map/while/body/eval_jaxpr/rgqd,kgd->rgqk/dot_general | solution.py:121
  230.6 5.7 %fusion.93 = f32[128,2,8]{0,2,1:T(8,128)S(1)} fusion(f32[2,1152,128,8]{2,1,3,0:T(8,128)} %get-tuple-element.490, f32[128,2,8]{0,2,1:T(8,128)S(1)} %select_maximum_fusion.2, pred[128,1152]{0,1:T(8,128)(4,1)S(1)} %compare_select_fusion.7), kind=kLoop, calls=%fused_computation.13.clone.1 | loop fusion | flops 9435136 | bytes 9601024 | tf_op jit(solution)/shard_map/while/body/eval_jaxpr/reduce_sum | solution.py:128
  237.0 4.3 %fusion.95 = f32[128,2,8,128]{0,3,2,1:T(8,128)} fusion(bf16[1152,2,128,1]{0,2,3,1:T(8,128)(2,1)S(1)} %bitcast.194, f32[2,1152,128,8]{2,1,3,0:T(8,128)S(1)} %copy-done, f32[128,2,8]{0,2,1:T(8,128)S(1)} %select_maximum_fusion.2, pred[128,1152]{0,1:T(8,128)(4,1)S(1)} %compare_select_fusion.7, f32[128,2,8,128]{0,3,2,1:T(8,128)} %get-tuple-element.544, ...), kind=kOutput, calls=%fused_computation.17.clone.1 | convolution fusion | flops 614203392 | bytes 12288001 | tf_op jit(solution)/shard_map/while/body/eval_jaxpr/rgqk,kgd->rgqd/dot_general | solution.py:129
  243.1 0.7 iota_compare_fusion.8
  243.8 1.1 compare_select_fusion.7
  244.9 1.3 constant_dynamic-slice_fusion.10
  246.3 5.3 %fusion.92 = (f32[128,2,8]{0,2,1:T(8,128)S(1)}, f32[2,1152,128,8]{2,1,3,0:T(8,128)}) fusion(pred[128,1152]{0,1:T(8,128)(4,1)S(1)} %compare_select_fusion.7, bf16[1152,2,128,1]{0,2,3,1:T(8,128)(2,1)S(1)} %bitcast.193, bf16[128,2,8,128]{3,2,1,0:T(8,128)(2,1)S(1)} %bitcast.191), kind=kOutput, calls=%fused_computation.9.clone.1 | convolution fusion | flops 611055616 | bytes 10706944 | tf_op jit(solution)/shard_map/while/body/eval_jaxpr/rgqd,kgd->rgqk/dot_general | solution.py:121
  251.6 5.7 %fusion.93 = f32[128,2,8]{0,2,1:T(8,128)S(1)} fusion(f32[2,1152,128,8]{2,1,3,0:T(8,128)} %get-tuple-element.490, f32[128,2,8]{0,2,1:T(8,128)S(1)} %select_maximum_fusion.2, pred[128,1152]{0,1:T(8,128)(4,1)S(1)} %compare_select_fusion.7), kind=kLoop, calls=%fused_computation.13.clone.1 | loop fusion | flops 9435136 | bytes 9601024 | tf_op jit(solution)/shard_map/while/body/eval_jaxpr/reduce_sum | solution.py:128
  258.0 4.3 %fusion.95 = f32[128,2,8,128]{0,3,2,1:T(8,128)} fusion(bf16[1152,2,128,1]{0,2,3,1:T(8,128)(2,1)S(1)} %bitcast.194, f32[2,1152,128,8]{2,1,3,0:T(8,128)S(1)} %copy-done, f32[128,2,8]{0,2,1:T(8,128)S(1)} %select_maximum_fusion.2, pred[128,1152]{0,1:T(8,128)(4,1)S(1)} %compare_select_fusion.7, f32[128,2,8,128]{0,3,2,1:T(8,128)} %get-tuple-element.544, ...), kind=kOutput, calls=%fused_computation.17.clone.1 | convolution fusion | flops 614203392 | bytes 12288001 | tf_op jit(solution)/shard_map/while/body/eval_jaxpr/rgqk,kgd->rgqd/dot_general | solution.py:129
  262.2 1.3 broadcast_divide_fusion
  263.8 1.0 select_convert_fusion
  (167 shorter events, 20.2 us)
Async XLA Ops:
  0.6 24.0 %copy-start.3 = (bf16[1,32,2,32,256]{4,3,2,1,0:T(8,128)(2,1)S(1)}, bf16[1,32,2,32,256]{4,3,2,1,0:T(8,128)(2,1)}, u32[]{:S(2)}) copy-start(bf16[1,32,2,32,256]{4,3,2,1,0:T(8,128)(2,1)} %param.18) | copy-start | bytes 3145732
  9.1 29.2 %all-to-all-start = ((bf16[32,2,16,256]{3,2,1,0:T(8,128)(2,1)}), bf16[32,2,16,256]{3,2,1,0:T(8,128)(2,1)S(1)}, u32[]{:S(2)}, u32[]{:S(2)}) async-start(bf16[32,2,16,256]{3,2,1,0:T(8,128)(2,1)} %scatter_fusion), calls=%async_computation | async-start | bytes 1048576 | tf_op jit(solution)/shard_map/all_to_all | solution.py:88
  24.7 24.0 %copy-start.10 = (f32[1,32,512]{2,1,0:T(8,128)S(1)}, f32[1,32,512]{2,1,0:T(8,128)}, u32[]{:S(2)}) copy-start(f32[1,32,512]{2,1,0:T(8,128)} %param.27) | copy-start | bytes 196612
  24.7 24.0 %copy-start.4 = (bf16[1,32,16,512]{3,2,1,0:T(8,128)(2,1)S(1)}, bf16[1,32,16,512]{3,2,1,0:T(8,128)(2,1)}, u32[]{:S(2)}) copy-start(bf16[1,32,16,512]{3,2,1,0:T(8,128)(2,1)} %param.24) | copy-start | bytes 1572868
  24.7 24.2 %copy-start.5 = (bf16[1,2,256,512]{3,2,1,0:T(8,128)(2,1)S(1)}, bf16[1,2,256,512]{3,2,1,0:T(8,128)(2,1)}, u32[]{:S(2)}) copy-start(bf16[1,2,256,512]{3,2,1,0:T(8,128)(2,1)} %param.25) | copy-start | bytes 1572868
  29.6 19.5 %copy-start.6 = (bf16[1,2,256,512]{3,2,1,0:T(8,128)(2,1)S(1)}, bf16[1,2,256,512]{3,2,1,0:T(8,128)(2,1)}, u32[]{:S(2)}) copy-start(bf16[1,2,256,512]{3,2,1,0:T(8,128)(2,1)} %param.26) | copy-start | bytes 1572868
  29.6 19.7 %copy-start.11 = (s32[1,1024]{1,0:T(1,128)S(1)}, s32[1,1024]{1,0:T(1,128)}, u32[]{:S(2)}) copy-start(s32[1,1024]{1,0:T(1,128)} %param.20) | copy-start | bytes 12292
  29.6 19.7 %copy-start.13 = (s32[1,1024]{1,0:T(1,128)S(1)}, s32[1,1024]{1,0:T(1,128)}, u32[]{:S(2)}) copy-start(s32[1,1024]{1,0:T(1,128)} %param.21) | copy-start | bytes 12292
  29.6 24.1 %copy-start.14 = (f32[32]{0:T(128)S(1)}, f32[32]{0:T(128)}, u32[]{:S(2)}) copy-start(f32[32]{0:T(128)} %param.28) | copy-start | bytes 388
  38.3 73.2 %all-to-all-start.1 = ((bf16[32,2,2,32,256]{4,3,2,1,0:T(8,128)(2,1)}), bf16[32,2,2,32,256]{4,3,2,1,0:T(8,128)(2,1)}, u32[]{:S(2)}, u32[]{:S(2)}) async-start(bf16[32,2,2,32,256]{4,3,2,1,0:T(8,128)(2,1)} %scatter_fusion.1), calls=%async_computation.1 | async-start | bytes 4194304 | tf_op jit(solution)/shard_map/all_to_all | solution.py:87
  48.8 65.0 %copy-start.9 = (bf16[1,2,128,256]{3,2,1,0:T(8,128)(2,1)S(1)}, bf16[1,2,128,256]{3,2,1,0:T(8,128)(2,1)}, u32[]{:S(2)}) copy-start(bf16[1,2,128,256]{3,2,1,0:T(8,128)(2,1)} %param.31) | copy-start | bytes 393220
  119.3 5.2 %copy-start.12 = (f32[32]{0:T(128)S(1)}, f32[32]{0:T(128)}, u32[]{:S(2)}) copy-start(f32[32]{0:T(128)} %param.29) | copy-start | bytes 388
  119.3 59.9 %all-to-all-start.2 = ((bf16[4,2,1152,256]{2,3,1,0:T(8,128)(2,1)}), bf16[4,2,1152,256]{2,3,1,0:T(8,128)(2,1)}, u32[]{:S(2)}, u32[]{:S(2)}) async-start(bf16[4,2,1152,256]{2,3,1,0:T(8,128)(2,1)} %stack.2), calls=%async_computation.2 | async-start | bytes 9437184 | tf_op jit(solution)/shard_map/all_to_all | solution.py:155
  124.5 54.7 %copy-start.2 = (bf16[1,128,2048]{2,1,0:T(8,128)(2,1)S(1)}, bf16[1,128,2048]{2,1,0:T(8,128)(2,1)}, u32[]{:S(2)}) copy-start(bf16[1,128,2048]{2,1,0:T(8,128)(2,1)} %param.30) | copy-start | bytes 1572868
  128.0 1.0 copy-start.7
  131.4 0.8 copy-start.8
  139.9 1.0 copy-start.7
  143.4 0.8 copy-start.8
  151.8 1.0 copy-start.7
  155.3 0.8 copy-start.8
  163.7 1.0 copy-start.7
  167.2 0.8 copy-start.8
  172.2 7.0 %copy-start.1 = (f32[32,16,256]{2,1,0:T(8,128)}, f32[32,16,256]{2,1,0:T(8,128)S(1)}, u32[]{:S(2)}) copy-start(f32[32,16,256]{2,1,0:T(8,128)S(1)} %get-tuple-element.235) | copy-start | bytes 1572868
  189.8 6.4 %copy-start = (f32[2,1152,128,8]{2,1,3,0:T(8,128)S(1)}, f32[2,1152,128,8]{2,1,3,0:T(8,128)}, u32[]{:S(2)}) copy-start(f32[2,1152,128,8]{2,1,3,0:T(8,128)} %get-tuple-element.490) | copy-start | bytes 28311556 | tf_op jit(solution)/shard_map/while
  209.6 6.4 %copy-start = (f32[2,1152,128,8]{2,1,3,0:T(8,128)S(1)}, f32[2,1152,128,8]{2,1,3,0:T(8,128)}, u32[]{:S(2)}) copy-start(f32[2,1152,128,8]{2,1,3,0:T(8,128)} %get-tuple-element.490) | copy-start | bytes 28311556 | tf_op jit(solution)/shard_map/while
  230.6 6.4 %copy-start = (f32[2,1152,128,8]{2,1,3,0:T(8,128)S(1)}, f32[2,1152,128,8]{2,1,3,0:T(8,128)}, u32[]{:S(2)}) copy-start(f32[2,1152,128,8]{2,1,3,0:T(8,128)} %get-tuple-element.490) | copy-start | bytes 28311556 | tf_op jit(solution)/shard_map/while
  251.6 6.4 %copy-start = (f32[2,1152,128,8]{2,1,3,0:T(8,128)S(1)}, f32[2,1152,128,8]{2,1,3,0:T(8,128)}, u32[]{:S(2)}) copy-start(f32[2,1152,128,8]{2,1,3,0:T(8,128)} %get-tuple-element.490) | copy-start | bytes 28311556 | tf_op jit(solution)/shard_map/while
